TPU v7x, 512 devices: a whole 4x4x16 slice. The times are simulated.
512 devices in a mesh: sec: 4 (over z_hi), dev: 128 (over z_lo, y, x, core).
Axes of the slice: x: 4, y: 4, z: 16 (z_hi: 4, z_lo: 4; z = z_hi * 4 + z_lo), core: 2. Of those that a mesh axis runs over, the one named last changes fastest.
Arguments:
- queries: bfloat16 [256, 8192], P('dev', 'sec'), may hold values from -24 to 24
- cache_keys: bfloat16 [256, 4, 512, 128], P('dev', 'sec'), may hold values from -24 to 24
- cache_values: bfloat16 [256, 4, 512, 128], P('dev', 'sec'), may hold values from -48 to 48
- lengths: int32 [256], P('dev'), may hold values from 2 to 512, as said below
- out_proj: bfloat16 [4096, 8192], P('dev', 'sec'), may hold values from -0.0625 to 0.0625
- residual: bfloat16 [256, 4096], P(None, 'dev'), may hold values from -3 to 3
- norm_gain: bfloat16 [4096], replicated, may hold values from 0.5 to 1.5
- expert_ids: int32 [256, 8], replicated, may hold values from 0 to 127, all different within a row; in each aligned block of 256 rows (0 to 255, 256 to 511, ...) at most 48 rows name the same one
- gate_weights: float32 [256, 8], replicated, may hold values from 0.5 to 1.5
- owners: int32 [128], replicated, may hold values from 0 to 127, each once
- gate_proj: bfloat16 [128, 768, 4096], P('dev', 'sec'), may hold values from -0.09375 to 0.09375
- up_proj: bfloat16 [128, 768, 4096], P('dev', 'sec'), may hold values from -0.09375 to 0.09375
- down_proj: bfloat16 [128, 768, 4096], P('dev', 'sec'), may hold values from -0.21875 to 0.21875
Outputs:
- output: bfloat16 [256, 4096], P(None, 'dev')
Inputs may be any that keep to these rules, and one draw needn't show every extreme that they name: Row r's cache holds lengths[r] live positions from position 0; some row holds exactly 512. `expert_ids`: each row names 8 different experts; over all 256 rows no expert is named more than 48 times, a bound that some block reaches. Each index appears once; expert e's projections stand at index owners[e] of the expert projections.
All inputs are finite; a program needn't handle non-finite values.
Results may differ from a plain program's by a relative error of at most 0.009.
Values may be sent and summed in bfloat16 or wider, within the bound.
No kernel may reach another device: no remote copies, remote signals or barrier semaphores. Data moves between devices by JAX's collectives and lax.ppermute only.
A program may use at most 64 MiB of HBM per device.

v0:
```python
import math
import jax
import jax.numpy as jnp
from jax import lax
from jax.sharding import PartitionSpec as P

epsilon = 1e-05


def slot_targets(expert_ids, owners, capacity):
    experts = owners.shape[0]
    flat_ids = expert_ids.reshape(-1)
    one_hot = (flat_ids[:, None] == jnp.arange(experts, dtype=jnp.int32)[None, :]).astype(jnp.int32)
    before = jnp.cumsum(one_hot, axis=0) - one_hot
    position = jnp.sum(before * one_hot, axis=1)
    holder = jnp.sum(one_hot * owners[None, :], axis=1)
    return (holder * capacity + position).reshape(expert_ids.shape)


def routing_tables(expert_ids, gate_weights, owners, capacity):
    target = slot_targets(expert_ids, owners, capacity)
    places = jnp.arange(owners.shape[0] * capacity, dtype=jnp.int32)
    matched = target[None, :, :] == places[:, None, None]
    sending = jnp.any(matched, axis=2)
    weighting = jnp.sum(
        jnp.where(matched, gate_weights[None, :, :], jnp.zeros_like(gate_weights)[None, :, :]),
        axis=2,
    )
    return (sending, weighting)


def times_transpose(left, right):
    return lax.dot_general(
        left, right, (((1,), (1,)), ((), ())), preferred_element_type=jnp.float32
    )


def attend(queries, cache_keys, cache_values, lengths):
    rows, kv_heads, key_span, head_dim = cache_keys.shape
    group_size = queries.shape[1] // (kv_heads * head_dim)
    grouped = queries.reshape(rows, kv_heads, group_size, head_dim)
    scores = jnp.einsum(
        "rkgd,rktd->rkgt", grouped, cache_keys, preferred_element_type=jnp.float32
    ) / math.sqrt(head_dim)
    live_mask = (
        jnp.arange(key_span, dtype=jnp.int32)[None, None, None, :] < lengths[:, None, None, None]
    )
    scores = jnp.where(live_mask, scores, -jnp.inf)
    row_top = jnp.max(scores, axis=-1, keepdims=True)
    raised = jnp.exp(scores - row_top)
    soft_weight = (raised / jnp.sum(raised, axis=-1, keepdims=True)).astype(jnp.bfloat16)
    head_out = jnp.einsum(
        "rkgt,rktd->rkgd", soft_weight, cache_values, preferred_element_type=jnp.float32
    )
    return head_out.astype(jnp.bfloat16).reshape(rows, -1)


def root_norm(arrived, norm_gain):
    square_mean = jnp.mean(arrived * arrived, axis=-1, keepdims=True)
    return (arrived * lax.rsqrt(square_mean + epsilon) * norm_gain.astype(jnp.float32)).astype(
        jnp.bfloat16
    )


def expert_ffn(normed, gate_w, up_w, down_w):
    gate_act = times_transpose(normed, gate_w)
    up_act = times_transpose(normed, up_w)
    hidden = (jax.nn.silu(gate_act) * up_act).astype(jnp.bfloat16)
    return jnp.dot(hidden, down_w, preferred_element_type=jnp.float32)


def shards(
    queries,
    cache_keys,
    cache_values,
    lengths,
    out_proj,
    residual,
    norm_gain,
    expert_ids,
    gate_weights,
    owners,
    gate_proj,
    up_proj,
    down_proj,
):
    head_out = attend(queries, cache_keys, cache_values, lengths)
    attention_part = times_transpose(lax.all_gather(head_out, "dev", axis=0, tiled=True), out_proj)
    rows_all, top_count = expert_ids.shape
    experts = owners.shape[0]
    capacity = min(rows_all, 3 * top_count * rows_all // experts)
    col_count = out_proj.shape[0]
    sending, weighting = routing_tables(expert_ids, gate_weights, owners, capacity)
    residual_wide = residual.astype(jnp.float32)
    attention_out = lax.psum(attention_part, "sec")
    hidden_in = (residual_wide + attention_out).astype(jnp.bfloat16)
    outbound = jnp.dot(sending.astype(jnp.bfloat16), hidden_in, preferred_element_type=jnp.float32)
    outbound = outbound.astype(jnp.bfloat16).reshape(experts, capacity, col_count)
    inbound = lax.all_to_all(outbound, "dev", split_axis=0, concat_axis=2, tiled=True)
    arrived = inbound[0].astype(jnp.float32)
    normed = root_norm(arrived, norm_gain)
    expert_out = expert_ffn(normed, gate_proj[0], up_proj[0], down_proj[0])
    place_weight = jnp.sum(weighting, axis=1)
    own_weight = lax.dynamic_slice_in_dim(
        place_weight, lax.axis_index("dev") * capacity, capacity, 0
    )
    weighted = (expert_out * own_weight[:, None]).astype(jnp.bfloat16)
    returned = lax.all_to_all(
        weighted.reshape(1, capacity, weighted.shape[1]),
        "dev",
        split_axis=2,
        concat_axis=0,
        tiled=True,
    )
    moe = jnp.dot(
        sending.T.astype(jnp.bfloat16),
        returned.reshape(-1, col_count),
        preferred_element_type=jnp.float32,
    )
    summed = lax.psum(moe, "sec")
    return (residual_wide + attention_out + summed).astype(jnp.bfloat16)


def solution(mesh):
    in_specs = (
        P("dev", "sec"),
        P("dev", "sec", None, None),
        P("dev", "sec", None, None),
        P("dev"),
        P("dev", "sec"),
        P(None, "dev"),
        P(),
        P(),
        P(),
        P(),
        P("dev", "sec", None),
        P("dev", "sec", None),
        P("dev", "sec", None),
    )
    out_specs = P(None, "dev")
    return jax.shard_map(shards, mesh=mesh, in_specs=in_specs, out_specs=out_specs, check_vma=False)
```

profile of v0, /device:TPU:8, one launch (start us, length us, event | category | flops | bytes accessed | tf_op | source)
XLA Modules:
  0.0 469.7 jit_solution(8240193825732816085)
XLA Ops:
  6.5 0.8 iota_compare_fusion.4
  7.4 1.1 fusion.14
  8.5 0.2 fusion.43
  8.7 1.2 convolution_convert_fusion.1
  9.9 0.6 reshape.152
  10.5 0.8 copy.33
  11.4 0.1 eq.42
  11.5 0.1 eq.38
  11.6 0.1 copy.35
  11.7 0.3 fusion.23
  12.1 0.1 broadcast_add_fusion
  12.2 0.3 copy.36
  12.5 0.3 copy-done.9
  12.8 1.1 select_reduce_fusion.1
  13.9 0.1 add.41
  14.1 57.2 %fusion.1 = pred[6144,256]{1,0:T(8,128)(4,1)} fusion(s32[256,8]{0,1:T(8,128)S(1)} %copy.37), kind=kLoop, calls=%fused_computation.3 | loop fusion | flops 23592960 | bytes 1581056 | tf_op jit(solution)/shard_map/reduce_or | solution.py:24
  71.3 146.4 %all-gather.3.cloned.1.call-done = bf16[128,2,2048]{2,1,0:T(2,128)(2,1)} async-done(((bf16[1,2,2048]{2,1,0:T(2,128)(2,1)}), bf16[128,2,2048]{2,1,0:T(2,128)(2,1)}) %all-gather.3.cloned.1.call-update) | async-done | bytes 1048592 | tf_op jit(solution)/shard_map/all_gather | solution.py:88
  217.7 1.5 reshape.153
  219.2 0.4 fusion.44
  219.6 25.8 %psum.14 = f32[256,32]{0,1:T(8,128)S(1)} all-reduce(f32[256,32]{0,1:T(8,128)S(1)} %fusion.44), channel_id=1, replica_groups=mesh['sec'=4,'dev'=128] {'sec'}, use_global_device_ids=true, to_apply=%region_2.3 | all-reduce | flops 8192 | bytes 65536 | tf_op jit(solution)/shard_map/psum | solution.py:95
  245.5 0.6 copy-done.5
  246.1 2.4 convolution_convert_fusion
  248.5 1.1 reshape.147
  249.6 1.7 copy.50
  251.3 3.4 reshape.155
  254.7 9.2 %all-to-all-start = ((bf16[128,2,768]{2,1,0:T(2,128)(2,1)}), bf16[128,2,768]{2,1,0:T(2,128)(2,1)S(1)}, u32[]{:S(2)}, u32[]{:S(2)}) async-start(bf16[128,2,768]{2,1,0:T(2,128)(2,1)} %reshape.155), calls=%async_computation | async-start | bytes 786432 | tf_op jit(solution)/shard_map/all_to_all | solution.py:99
  263.9 0.1 reshape.151
  264.0 91.4 %select_reduce_fusion = f32[6144]{0:T(1024)S(1)} fusion(f32[256,8]{0,1:T(8,128)S(1)} %copy-done.10, s32[256,8]{0,1:T(8,128)S(1)} %copy.37), kind=kLoop, calls=%fused_computation.1 | loop fusion | flops 37742592 | bytes 40960 | tf_op jit(solution)/shard_map/reduce_sum | solution.py:103
  355.4 0.6 dynamic_slice.3
  356.0 1.0 reshape.156
  357.0 0.6 fusion.4
  357.6 0.7 fusion.6
  358.3 1.0 copy-done.1
  359.3 1.2 fusion.10
  360.4 2.5 fusion.3
  362.9 3.9 copy.40
  366.8 0.5 broadcast.89
  367.3 23.6 %reduce.7 = bf16[4096,48]{1,0:T(8,128)(2,1)S(1)} reduce(bf16[4096,1,48]{2,1,0:T(2,128)(2,1)} %bitcast.71, bf16[]{:T(256)} %broadcast.89), dimensions={1}, to_apply=%bitcast.53.reduce_sub_computation | reduce | bytes 786434
  390.9 1.4 reshape.157
  392.3 27.2 %all_to_all.24 = bf16[128,2,768]{2,1,0:T(2,128)(2,1)S(1)} all-to-all(bf16[128,2,768]{2,1,0:T(2,128)(2,1)S(1)} %reshape.157), channel_id=1, replica_groups=mesh['sec'=4,'dev'=128] {'dev'}, dimensions={0} | all-to-all | bytes 786432 | tf_op jit(solution)/shard_map/all_to_all | solution.py:108
  419.5 4.1 reshape.158
  423.6 4.6 copy.41
  428.1 1.3 all_to_all.20
  429.4 3.4 copy.42
  432.8 2.8 reshape.149
  435.6 2.3 fusion.45
  437.9 24.1 %psum.15 = f32[256,32]{0,1:T(8,128)S(1)} all-reduce(f32[256,32]{0,1:T(8,128)S(1)} %fusion.45), channel_id=1, replica_groups=mesh['sec'=4,'dev'=128] {'sec'}, use_global_device_ids=true, to_apply=%region_10.11 | all-reduce | flops 8192 | bytes 65536 | tf_op jit(solution)/shard_map/psum | solution.py:120
  462.0 0.6 add_convert_fusion
  (28 shorter events, 0.2 us)
Async XLA Ops:
  6.5 353.9 %copy-start = (bf16[1,192,4096]{2,1,0:T(8,128)(2,1)S(1)}, bf16[1,192,4096]{2,1,0:T(8,128)(2,1)}, u32[]{:S(2)}) copy-start(bf16[1,192,4096]{2,1,0:T(8,128)(2,1)} %param.25) | copy-start | bytes 4718596
  6.5 211.2 %all-gather.3.cloned.1.call-start = ((), (), s32[]{:S(2)}) async-start(), calls=%async_computation.2 | async-start | bytes 1056768 | tf_op jit(solution)/shard_map/all_gather | solution.py:88
  12.2 0.7 copy-start.9
  14.1 205.1 %copy-start.4 = (bf16[32,2048]{1,0:T(8,128)(2,1)S(1)}, bf16[32,2048]{1,0:T(8,128)(2,1)}, u32[]{:S(2)}) copy-start(bf16[32,2048]{1,0:T(8,128)(2,1)} %param.17) | copy-start | bytes 393220
  71.3 174.8 %copy-start.7 = (bf16[256,32]{0,1:T(8,128)(2,1)S(1)}, bf16[256,32]{0,1:T(8,128)(2,1)}, u32[]{:S(2)}) copy-start(bf16[256,32]{0,1:T(8,128)(2,1)} %param.18) | copy-start | bytes 49156
  245.5 0.6 copy-start.5
  251.3 12.6 %copy-start.8 = (bf16[4096]{0:T(1024)(128)(2,1)S(1)}, bf16[4096]{0:T(1024)(128)(2,1)}, u32[]{:S(2)}) copy-start(bf16[4096]{0:T(1024)(128)(2,1)} %param.19) | copy-start | bytes 24580
  251.3 12.7 %copy-start.10 = (f32[256,8]{0,1:T(8,128)S(1)}, f32[256,8]{0,1:T(8,128)}, u32[]{:S(2)}) copy-start(f32[256,8]{0,1:T(8,128)} %param.21) | copy-start | bytes 24580
  254.7 101.3 %all-to-all-start = ((bf16[128,2,768]{2,1,0:T(2,128)(2,1)}), bf16[128,2,768]{2,1,0:T(2,128)(2,1)S(1)}, u32[]{:S(2)}, u32[]{:S(2)}) async-start(bf16[128,2,768]{2,1,0:T(2,128)(2,1)} %reshape.155), calls=%async_computation | async-start | bytes 786432 | tf_op jit(solution)/shard_map/all_to_all | solution.py:99
  357.0 2.3 copy-start.2
  358.3 1.0 copy-start.1
  358.3 2.2 copy-start.3
  435.5 26.4 %copy-start.6 = (f32[256,32]{0,1:T(8,128)S(1)}, f32[256,32]{0,1:T(8,128)}, u32[]{:S(2)}) copy-start(f32[256,32]{0,1:T(8,128)} %copy-done.5) | copy-start | bytes 98308
Sparse Core Ops, SparseCore 0:
  10.7 207.0 all-gather.2
where the time goes:
time: 476 us; the launch traced here: 470 us
  other arithmetic  177 us (37%)
  waiting for transfers between devices  146 us (31%)
  blocking collectives  77.1 us (16%)
  local copies, waits for them, and re-layouts  35.3 us (7%)
  between operations  13.9 us (3%)
  matrix products  11.1 us (2%)
  starting transfers between devices  9.19 us (2%)
    all_gather x1, waiting for transfers between devices, shards(): lax.all_gather(head_out, 'dev', axis=0, tiled=True)  146 us
    reduce_sum x1, other arithmetic, shards(): place_weight = jnp.sum(weighting, axis=1)  91.4 us
    reduce_or x1, other arithmetic, routing_tables(): sending = jnp.any(matched, axis=2)  57.2 us
    all_to_all x1, blocking collectives, shards(): lax.all_to_all(weighted.reshape(1, capacity, weighted.shape[1]), 'dev', s...  27.2 us
    psum x1, blocking collectives, shards(): attention_out = lax.psum(attention_part, 'sec')  25.8 us
    psum x1, blocking collectives, shards(): summed = lax.psum(moe, 'sec')  24.1 us
    unnamed x1, other arithmetic  23.6 us
    unnamed x30, local copies, waits for them, and re-layouts  15.2 us
  transfers between devices with their start and end apart: 2, of which 1 were waited for; matrix products, arithmetic and copies ran while one was open for 32% of the time, Pallas kernels for 0%

commit v1 on v0

--- a/solution.py
+++ b/solution.py
@@ -105,13 +105,11 @@
         place_weight, lax.axis_index("dev") * capacity, capacity, 0
     )
     weighted = (expert_out * own_weight[:, None]).astype(jnp.bfloat16)
-    returned = lax.all_to_all(
-        weighted.reshape(1, capacity, weighted.shape[1]),
-        "dev",
-        split_axis=2,
-        concat_axis=0,
-        tiled=True,
-    )
+    own = weighted.reshape(1, capacity, weighted.shape[1])
+    size = lax.axis_size("dev")
+    blocks = jnp.stack(jnp.split(own, size, axis=2), axis=0)
+    blocks = lax.all_to_all(blocks, "dev", split_axis=0, concat_axis=0)
+    returned = jnp.concatenate(blocks, axis=0)
     moe = jnp.dot(
         sending.T.astype(jnp.bfloat16),
         returned.reshape(-1, col_count),

time: 476 us -> 516 us (1.084); the launches traced: 470 us -> 515 us
  local copies, waits for them, and re-layouts: 35.3 us -> 106 us
  other arithmetic: 177 us -> 153 us
    unnamed x30 -> x156, local copies, waits for them, and re-layouts: 15.2 us -> 94.9 us
    unnamed x1 -> x0, other arithmetic: 23.6 us -> none
    all_to_all x3 -> x1, local copies, waits for them, and re-layouts: 9.21 us -> 1.37 us  [shards(): blocks = lax.all_to_all(blocks, 'dev', split_axis=0, concat_axis=0)]
    reshape x2 -> x0, local copies, waits for them, and re-layouts: 6.62 us -> none  [the longest x1 3.86 us: shards(): weighted.reshape(1, capacity, weighted.shape[1])]
    another operation x3 -> x6, local copies, waits for them, and re-layouts: 0.35 us -> 5.84 us  [the longest x1 2.77 us: shards(): returned.reshape(-1, col_count)]
  transfers between devices with their start and end apart: 2 -> 2, of which waited for: 1 -> 1; matrix products, arithmetic and copies ran while one was open for 32% -> 30% of each run, Pallas kernels for 0% -> 0%
where the time goes in v1:
time: 516 us; the launch traced here: 515 us
  other arithmetic  153 us (30%)
  waiting for transfers between devices  146 us (28%)
  local copies, waits for them, and re-layouts  106 us (21%)
  blocking collectives  76.5 us (15%)
  between operations  13.7 us (3%)
  matrix products  11.1 us (2%)
  starting transfers between devices  8.56 us (2%)
    all_gather x1, waiting for transfers between devices, shards(): lax.all_gather(head_out, 'dev', axis=0, tiled=True)  146 us
    unnamed x156, local copies, waits for them, and re-layouts  94.9 us
    reduce_sum x1, other arithmetic, shards(): place_weight = jnp.sum(weighting, axis=1)  91.4 us
    reduce_or x1, other arithmetic, routing_tables(): sending = jnp.any(matched, axis=2)  57.2 us
    all_to_all x1, blocking collectives, shards(): blocks = lax.all_to_all(blocks, 'dev', split_axis=0, concat_axis=0)  27 us
    psum x1, blocking collectives, shards(): attention_out = lax.psum(attention_part, 'sec')  25.4 us
    psum x1, blocking collectives, shards(): summed = lax.psum(moe, 'sec')  24.1 us
  transfers between devices with their start and end apart: 2, of which 1 were waited for; matrix products, arithmetic and copies ran while one was open for 30% of the time, Pallas kernels for 0%

profile of v1, /device:TPU:8, one launch (start us, length us, event | category | flops | bytes accessed | tf_op | source)
XLA Modules:
  0.0 515.3 jit_solution(7048621202383778954)
XLA Ops:
  6.5 0.8 iota_compare_fusion.4
  7.4 1.1 fusion.14
  8.7 1.2 convolution_convert_fusion.1
  10.5 0.8 copy.295
  12.8 1.1 select_reduce_fusion.1
  14.1 57.2 %fusion.1 = pred[6144,256]{1,0:T(8,128)(4,1)} fusion(s32[256,8]{0,1:T(8,128)S(1)} %copy.299), kind=kLoop, calls=%fused_computation.3 | loop fusion | flops 23592960 | bytes 1581056 | tf_op jit(solution)/shard_map/reduce_or | solution.py:24
  71.3 146.4 %all-gather.3.cloned.1.call-done = bf16[128,2,2048]{2,1,0:T(2,128)(2,1)} async-done(((bf16[1,2,2048]{2,1,0:T(2,128)(2,1)}), bf16[128,2,2048]{2,1,0:T(2,128)(2,1)}) %all-gather.3.cloned.1.call-update) | async-done | bytes 1048592 | tf_op jit(solution)/shard_map/all_gather | solution.py:88
  217.7 1.5 reshape.148
  219.6 25.4 %psum.14 = f32[256,32]{0,1:T(8,128)S(1)} all-reduce(f32[256,32]{0,1:T(8,128)S(1)} %fusion.44), channel_id=1, replica_groups=mesh['sec'=4,'dev'=128] {'sec'}, use_global_device_ids=true, to_apply=%region_2.3 | all-reduce | flops 8192 | bytes 65536 | tf_op jit(solution)/shard_map/psum | solution.py:95
  245.7 2.4 convolution_convert_fusion
  248.1 1.1 reshape.143
  249.2 1.6 copy.311
  250.9 3.4 reshape.150
  254.3 8.6 %all-to-all-start = ((bf16[128,2,768]{2,1,0:T(2,128)(2,1)}), bf16[128,2,768]{2,1,0:T(2,128)(2,1)S(1)}, u32[]{:S(2)}, u32[]{:S(2)}) async-start(bf16[128,2,768]{2,1,0:T(2,128)(2,1)} %reshape.150), calls=%async_computation | async-start | bytes 786432 | tf_op jit(solution)/shard_map/all_to_all | solution.py:99
  262.9 91.4 %select_reduce_fusion = f32[6144]{0:T(1024)S(1)} fusion(f32[256,8]{0,1:T(8,128)S(1)} %copy-done.10, s32[256,8]{0,1:T(8,128)S(1)} %copy.299), kind=kLoop, calls=%fused_computation.1 | loop fusion | flops 37742592 | bytes 40960 | tf_op jit(solution)/shard_map/reduce_sum | solution.py:103
  354.9 1.0 reshape.151
  356.5 0.7 fusion.6
  357.3 0.9 copy-done.1
  358.2 1.2 fusion.10
  359.4 2.5 fusion.3
  373.6 0.7 constant_dynamic-update-slice_fusion.109
  378.9 0.7 constant_dynamic-update-slice_fusion.101
  381.5 0.7 constant_dynamic-update-slice_fusion.97
  382.2 0.7 constant_dynamic-update-slice_fusion.96
  389.4 0.7 constant_dynamic-update-slice_fusion.85
  391.3 0.7 constant_dynamic-update-slice_fusion.82
  392.7 0.7 constant_dynamic-update-slice_fusion.80
  394.6 0.7 constant_dynamic-update-slice_fusion.77
  399.9 0.7 constant_dynamic-update-slice_fusion.69
  400.6 0.7 constant_dynamic-update-slice_fusion.68
  402.5 0.7 constant_dynamic-update-slice_fusion.65
  405.1 0.7 constant_dynamic-update-slice_fusion.61
  409.7 0.7 constant_dynamic-update-slice_fusion.54
  410.4 0.7 constant_dynamic-update-slice_fusion.53
  416.3 0.7 constant_dynamic-update-slice_fusion.44
  422.8 0.7 constant_dynamic-update-slice_fusion.34
  426.8 0.7 constant_dynamic-update-slice_fusion.28
  428.1 0.7 constant_dynamic-update-slice_fusion.26
  434.0 0.7 constant_dynamic-update-slice_fusion.17
  441.9 0.7 constant_dynamic-update-slice_fusion.5
  445.8 2.1 copy.302
  447.9 1.4 reshape.152
  449.3 27.0 %all_to_all.14 = bf16[128,2,768]{2,1,0:T(2,128)(2,1)S(1)} all-to-all(bf16[128,2,768]{2,1,0:T(2,128)(2,1)S(1)} %reshape.152), channel_id=1, replica_groups=mesh['sec'=4,'dev'=128] {'dev'}, dimensions={0} | all-to-all | bytes 786432 | tf_op jit(solution)/shard_map/all_to_all | solution.py:111
  476.3 1.0 reshape.153
  477.3 1.4 copy.303
  478.7 2.8 reshape_reshape.3
  481.5 2.3 fusion.45
  483.8 24.1 %psum.15 = f32[256,32]{0,1:T(8,128)S(1)} all-reduce(f32[256,32]{0,1:T(8,128)S(1)} %fusion.45), channel_id=1, replica_groups=mesh['sec'=4,'dev'=128] {'sec'}, use_global_device_ids=true, to_apply=%region_10.11 | all-reduce | flops 8192 | bytes 65536 | tf_op jit(solution)/shard_map/psum | solution.py:118
  (152 shorter events, 75.6 us)
Async XLA Ops:
  6.5 352.8 %copy-start = (bf16[1,192,4096]{2,1,0:T(8,128)(2,1)S(1)}, bf16[1,192,4096]{2,1,0:T(8,128)(2,1)}, u32[]{:S(2)}) copy-start(bf16[1,192,4096]{2,1,0:T(8,128)(2,1)} %param.25) | copy-start | bytes 4718596
  6.5 211.2 %all-gather.3.cloned.1.call-start = ((), (), s32[]{:S(2)}) async-start(), calls=%async_computation.2 | async-start | bytes 1056768 | tf_op jit(solution)/shard_map/all_gather | solution.py:88
  12.2 0.7 copy-start.9
  14.1 205.1 %copy-start.4 = (bf16[32,2048]{1,0:T(8,128)(2,1)S(1)}, bf16[32,2048]{1,0:T(8,128)(2,1)}, u32[]{:S(2)}) copy-start(bf16[32,2048]{1,0:T(8,128)(2,1)} %param.17) | copy-start | bytes 393220
  71.3 174.4 %copy-start.7 = (bf16[256,32]{0,1:T(8,128)(2,1)S(1)}, bf16[256,32]{0,1:T(8,128)(2,1)}, u32[]{:S(2)}) copy-start(bf16[256,32]{0,1:T(8,128)(2,1)} %param.18) | copy-start | bytes 49156
  245.1 0.6 copy-start.5
  250.9 12.0 %copy-start.8 = (bf16[4096]{0:T(1024)(128)(2,1)S(1)}, bf16[4096]{0:T(1024)(128)(2,1)}, u32[]{:S(2)}) copy-start(bf16[4096]{0:T(1024)(128)(2,1)} %param.19) | copy-start | bytes 24580
  250.9 12.1 %copy-start.10 = (f32[256,8]{0,1:T(8,128)S(1)}, f32[256,8]{0,1:T(8,128)}, u32[]{:S(2)}) copy-start(f32[256,8]{0,1:T(8,128)} %param.21) | copy-start | bytes 24580
  254.3 100.6 %all-to-all-start = ((bf16[128,2,768]{2,1,0:T(2,128)(2,1)}), bf16[128,2,768]{2,1,0:T(2,128)(2,1)S(1)}, u32[]{:S(2)}, u32[]{:S(2)}) async-start(bf16[128,2,768]{2,1,0:T(2,128)(2,1)} %reshape.150), calls=%async_computation | async-start | bytes 786432 | tf_op jit(solution)/shard_map/all_to_all | solution.py:99
  356.0 2.3 copy-start.2
  357.2 1.0 copy-start.1
  357.3 2.1 copy-start.3
  481.4 26.4 %copy-start.6 = (f32[256,32]{0,1:T(8,128)S(1)}, f32[256,32]{0,1:T(8,128)}, u32[]{:S(2)}) copy-start(f32[256,32]{0,1:T(8,128)} %copy-done.5) | copy-start | bytes 98308
Sparse Core Ops, SparseCore 0:
  10.7 207.0 all-gather.2
